TPU v7x, 32 devices: a whole 2x2x4 slice. The times are simulated.
32 devices in a mesh: ctx: 16 (over z, y, x), fsdp: 2 (over core).
Axes of the slice: x: 2, y: 2, z: 4, core: 2. Of those that a mesh axis runs over, the one named last changes fastest.
Arguments:
- layer_input: bfloat16 [2, 2048, 4544], P('fsdp', 'ctx'), may hold values from -6 to 6
- cotangent: bfloat16 [2, 2048, 4544], P('fsdp', 'ctx'), may hold values from -6 to 6
- norm_gain: float32 [4544], replicated, may hold values from 0.5 to 1.5
- norm_bias: float32 [4544], replicated, may hold values from -3 to 3
- qkv_weight: bfloat16 [4544, 4672], P('ctx', 'fsdp'), may hold values from -1 to 1
- up_weight: bfloat16 [4544, 18176], P('ctx', 'fsdp'), may hold values from -0.09375 to 0.09375
- dense_weight: bfloat16 [4544, 4544], P('ctx', 'fsdp'), may hold values from -0.75 to 0.75
- down_weight: bfloat16 [4544, 18176], P('ctx', 'fsdp'), may hold values from -0.046875 to 0.046875
Outputs:
- layer_output: bfloat16 [2, 2048, 4544], P('fsdp', 'ctx')
- input_grad: float32 [2, 2048, 4544], P('fsdp', 'ctx')
- gain_grad: float32 [4544], replicated
- bias_grad: float32 [4544], replicated
- qkv_grad: float32 [4544, 4672], P('ctx', 'fsdp')
- up_grad: float32 [4544, 18176], P('ctx', 'fsdp')
- dense_grad: float32 [4544, 4544], P('ctx', 'fsdp')
- down_grad: float32 [4544, 18176], P('ctx', 'fsdp')
All inputs are finite; a program needn't handle non-finite values.
Results may differ from a plain program's by a relative error of at most 0.04.
Values may be sent and summed in bfloat16 or wider, within the bound.
A program may use at most 1.625 GiB of HBM per device.

v0:
```python
import math
import jax
import jax.numpy as jnp
from jax import lax
from jax.sharding import PartitionSpec as P

HEADS = 71
HEAD = 64
epsilon = 1e-05
rope_base = 10000.0
masked_score = -1e30


def in_blocks(shard, dim, size):
    shape = shard.shape
    blocks = shard.reshape(*shape[:dim], size, shape[dim] // size, *shape[dim + 1 :])
    return jnp.moveaxis(blocks, dim, 0)


def sent_and_summed(shard, axis, dim):
    size = lax.axis_size(axis)
    blocks = lax.all_to_all(in_blocks(shard, dim, size), axis, 0, 0, tiled=True)
    return jnp.sum(blocks.astype(jnp.float32), axis=0)


def layer_norm(values, gain_vec, bias_vec):
    center = values - jnp.mean(values, -1, keepdims=True)
    spread = jnp.mean(center * center, -1, keepdims=True)
    return center * lax.rsqrt(spread + epsilon) * gain_vec + bias_vec


def rotate(values, cosines, sines):
    middle = values.shape[-1] // 2
    turned = jnp.concatenate([-values[..., middle:], values[..., :middle]], -1)
    return values * cosines + turned * sines


def angles(positions, head_size):
    inverse_freq = rope_base ** (-jnp.arange(0, head_size, 2).astype(jnp.float32) / head_size)
    phases = positions.astype(jnp.float32)[:, None] * inverse_freq[None, :]
    phases = jnp.concatenate([phases, phases], -1)
    return (jnp.cos(phases), jnp.sin(phases))


def gather_halves(first, second):
    return (
        lax.all_gather(first, "fsdp", axis=1, tiled=True),
        lax.all_gather(second, "fsdp", axis=1, tiled=True),
    )


def grad_halves(partial_grad):
    return lax.psum_scatter(
        partial_grad.astype(jnp.bfloat16), "fsdp", scatter_dimension=1, tiled=True
    ).astype(jnp.float32)


def fold_inputs(left, first, second):
    return (
        jnp.dot(
            left,
            lax.all_gather(first, "ctx", axis=0, tiled=True),
            preferred_element_type=jnp.float32,
        ),
        jnp.dot(
            left,
            lax.all_gather(second, "ctx", axis=0, tiled=True),
            preferred_element_type=jnp.float32,
        ),
    )


def fold_outputs(first_left, second_left, first, second):
    contract = (((1,), (1,)), ((), ()))
    partial_term = lax.dot_general(
        first_left,
        lax.all_gather(first, "ctx", axis=0, tiled=True),
        contract,
        preferred_element_type=jnp.float32,
    )
    return partial_term + lax.dot_general(
        second_left,
        lax.all_gather(second, "ctx", axis=0, tiled=True),
        contract,
        preferred_element_type=jnp.float32,
    )


def grad_blocks(left, right):
    left_columns = lax.all_to_all(left, "ctx", split_axis=1, concat_axis=0, tiled=True)
    across = (((0,), (0,)), ((), ()))
    return lax.dot_general(
        left_columns,
        lax.all_gather(right, "ctx", axis=0, tiled=True),
        across,
        preferred_element_type=jnp.float32,
    )


def alternate(first, second, pair_count):
    row_total = first.shape[0]
    first_parts = first.reshape(row_total, pair_count, first.shape[1] // pair_count)
    second_parts = second.reshape(row_total, pair_count, second.shape[1] // pair_count)
    return jnp.concatenate([first_parts, second_parts], 2).reshape(row_total, -1)


def block_scores(query_block, keyvals, key_index, key_rows, query_pos, head_size):
    key_block = lax.dynamic_slice_in_dim(keyvals, key_index * key_rows, key_rows, 0)
    raw_scores = lax.dot_general(
        query_block,
        key_block[:, :head_size],
        (((1,), (1,)), ((), ())),
        preferred_element_type=jnp.float32,
    ) * head_size ** (-0.5)
    key_pos = key_index * key_rows + lax.iota(jnp.int32, key_rows)
    return (jnp.where(key_pos[None, :] <= query_pos[:, None], raw_scores, masked_score), key_block)


def attend_forward(queries, keyvals, offset, head_count, head_size):
    row_total = queries.shape[0]
    tokens = row_total // head_count
    query_tokens = math.gcd(32, tokens)
    key_rows = math.gcd(1024, keyvals.shape[0])
    block_rows = query_tokens * head_count
    blocks = queries.reshape(tokens // query_tokens, block_rows, head_size)
    numbers = jnp.arange(tokens // query_tokens, dtype=jnp.int32)

    def one_block(operands):
        query_block, number = operands
        query_pos = offset + number * query_tokens + lax.iota(jnp.int32, block_rows) // head_count
        key_blocks = (offset + (number + 1) * query_tokens + key_rows - 1) // key_rows

        def statistics(key_index, state_pair):
            row_max, exp_sum = state_pair
            scores, key_block = block_scores(
                query_block, keyvals, key_index, key_rows, query_pos, head_size
            )
            new_max = jnp.maximum(row_max, jnp.max(scores, 1))
            exp_sum = exp_sum * jnp.exp(row_max - new_max) + jnp.sum(
                jnp.exp(scores - new_max[:, None]), 1
            )
            return (new_max, exp_sum)

        start_state = (
            jnp.full((block_rows,), masked_score, jnp.float32),
            jnp.zeros((block_rows,), jnp.float32),
        )
        row_max, exp_sum = lax.fori_loop(0, key_blocks, statistics, start_state)

        def one_accumulate(key_index, output_sum):
            scores, key_block = block_scores(
                query_block, keyvals, key_index, key_rows, query_pos, head_size
            )
            probabilities = (jnp.exp(scores - row_max[:, None]) / exp_sum[:, None]).astype(
                jnp.bfloat16
            )
            return output_sum + jnp.dot(
                probabilities, key_block[:, head_size:], preferred_element_type=jnp.float32
            )

        output_sum = lax.fori_loop(
            0, key_blocks, one_accumulate, jnp.zeros((block_rows, head_size), jnp.float32)
        )
        return (output_sum, row_max, exp_sum)

    outputs, row_max, exp_sum = lax.map(one_block, (blocks, numbers))
    return (
        outputs.reshape(row_total, head_size),
        row_max.reshape(row_total),
        exp_sum.reshape(row_total),
    )


def attend_backward(
    queries, keyvals, grad_heads, delta, row_max, exp_sum, offset, head_count, head_size
):
    row_total = queries.shape[0]
    tokens = row_total // head_count
    query_tokens = math.gcd(32, tokens)
    key_rows = math.gcd(1024, keyvals.shape[0])
    block_rows = query_tokens * head_count
    block_count = tokens // query_tokens
    numbers = jnp.arange(block_count, dtype=jnp.int32)
    scale = head_size ** (-0.5)
    across = (((0,), (0,)), ((), ()))

    def one_block(keyval_grad, operands):
        query_block, grad_block, delta_block, max_block, sum_block, number = operands
        query_pos = offset + number * query_tokens + lax.iota(jnp.int32, block_rows) // head_count
        key_blocks = (offset + (number + 1) * query_tokens + key_rows - 1) // key_rows

        def step_back(key_index, state_pair):
            query_grad, keyval_grad = state_pair
            scores, key_block = block_scores(
                query_block, keyvals, key_index, key_rows, query_pos, head_size
            )
            probabilities = jnp.exp(scores - max_block[:, None]) / sum_block[:, None]
            prob_low = probabilities.astype(jnp.bfloat16)
            prob_grad = lax.dot_general(
                grad_block,
                key_block[:, head_size:],
                (((1,), (1,)), ((), ())),
                preferred_element_type=jnp.float32,
            )
            score_grad = (probabilities * (prob_grad - delta_block[:, None])).astype(jnp.bfloat16)
            query_grad = (
                query_grad
                + jnp.dot(score_grad, key_block[:, :head_size], preferred_element_type=jnp.float32)
                * scale
            )
            key_grad = (
                lax.dot_general(score_grad, query_block, across, preferred_element_type=jnp.float32)
                * scale
            )
            value_grad = lax.dot_general(
                prob_low, grad_block, across, preferred_element_type=jnp.float32
            )
            first_row = key_index * key_rows
            current = lax.dynamic_slice_in_dim(keyval_grad, first_row, key_rows, 0)
            keyval_grad = lax.dynamic_update_slice_in_dim(
                keyval_grad, current + jnp.concatenate([key_grad, value_grad], 1), first_row, 0
            )
            return (query_grad, keyval_grad)

        start_state = (jnp.zeros((block_rows, head_size), jnp.float32), keyval_grad)
        query_grad, keyval_grad = lax.fori_loop(0, key_blocks, step_back, start_state)
        return (keyval_grad, query_grad)

    operands = (
        queries.reshape(block_count, block_rows, head_size),
        grad_heads.reshape(block_count, block_rows, head_size),
        delta.reshape(block_count, block_rows),
        row_max.reshape(block_count, block_rows),
        exp_sum.reshape(block_count, block_rows),
        numbers,
    )
    start_grad = jnp.zeros((keyvals.shape[0], 2 * head_size), jnp.float32)
    keyval_grad, query_grads = lax.scan(one_block, start_grad, operands)
    return (query_grads.reshape(row_total, head_size), keyval_grad)


def body(
    layer_input, cotangent, norm_gain, norm_bias, qkv_weight, up_weight, dense_weight, down_weight
):
    head_size = HEAD
    head_count = HEADS
    inputs = layer_input[0].astype(jnp.float32)
    tokens = inputs.shape[0]
    features = inputs.shape[1]
    offset = lax.axis_index("ctx") * tokens
    pair_count = lax.axis_size("fsdp")
    normed = layer_norm(inputs, norm_gain, norm_bias)
    normed_low = normed.astype(jnp.bfloat16)
    whole_qkv, whole_up = gather_halves(qkv_weight, up_weight)
    joined_out, up_raw = fold_inputs(normed_low, whole_qkv, whole_up)
    cosines, sines = angles(offset + lax.iota(jnp.int32, tokens), head_size)
    query_raw = joined_out[:, :features].reshape(tokens, head_count, head_size)
    key_raw = joined_out[:, features : features + head_size]
    value_raw = joined_out[:, features + head_size :]
    query_rot = rotate(query_raw, cosines[:, None, :], sines[:, None, :]).astype(jnp.bfloat16)
    key_rot = rotate(key_raw, cosines, sines).astype(jnp.bfloat16)
    keyvals_mine = jnp.concatenate([key_rot, value_raw.astype(jnp.bfloat16)], 1)
    keyvals = lax.all_gather(keyvals_mine, "ctx", axis=0, tiled=True)
    queries = query_rot.reshape(tokens * head_count, head_size)
    attention, row_max, exp_sum = attend_forward(queries, keyvals, offset, head_count, head_size)
    attended_low = attention.reshape(tokens, features).astype(jnp.bfloat16)
    hidden_low = jax.nn.gelu(up_raw, approximate=False).astype(jnp.bfloat16)
    whole_dense, whole_down = gather_halves(dense_weight, down_weight)
    branch = fold_outputs(attended_low, hidden_low, whole_dense, whole_down)
    layer_output = (inputs + branch).astype(jnp.bfloat16)
    grad_low = cotangent[0]
    whole_dense, whole_down = gather_halves(dense_weight, down_weight)
    grad_attended, grad_hidden = fold_inputs(grad_low, whole_dense, whole_down)
    late_grads = grad_halves(grad_blocks(grad_low, alternate(attended_low, hidden_low, pair_count)))
    dense_cols = dense_weight.shape[1]
    dense_grad = late_grads[:, :dense_cols]
    down_grad = late_grads[:, dense_cols:]
    grad_heads = grad_attended.astype(jnp.bfloat16).reshape(tokens * head_count, head_size)
    delta = jnp.sum(grad_heads.astype(jnp.float32) * attention, 1)
    query_grad, keyval_grad = attend_backward(
        queries, keyvals, grad_heads, delta, row_max, exp_sum, offset, head_count, head_size
    )
    keyval_mine = sent_and_summed(keyval_grad.astype(jnp.bfloat16), "ctx", 0)
    _, query_back = jax.vjp(
        lambda vector: rotate(vector, cosines[:, None, :], sines[:, None, :]), query_raw
    )
    query_unrot = query_back(query_grad.reshape(tokens, head_count, head_size))[0]
    _, key_back = jax.vjp(lambda vector: rotate(vector, cosines, sines), key_raw)
    key_unrot = key_back(keyval_mine[:, :head_size])[0]
    grad_joined = jnp.concatenate(
        [query_unrot.reshape(tokens, features), key_unrot, keyval_mine[:, head_size:]], 1
    ).astype(jnp.bfloat16)
    _, gelu_back = jax.vjp(lambda vector: jax.nn.gelu(vector, approximate=False), up_raw)
    grad_up = gelu_back(grad_hidden)[0].astype(jnp.bfloat16)
    whole_qkv, whole_up = gather_halves(qkv_weight, up_weight)
    grad_normed = fold_outputs(grad_joined, grad_up, whole_qkv, whole_up)
    early_grads = grad_halves(grad_blocks(normed_low, alternate(grad_joined, grad_up, pair_count)))
    qkv_cols = qkv_weight.shape[1]
    qkv_grad = early_grads[:, :qkv_cols]
    up_grad = early_grads[:, qkv_cols:]
    _, norm_back = jax.vjp(layer_norm, inputs, norm_gain, norm_bias)
    input_part, gain_part, bias_part = norm_back(grad_normed)
    gain_grad, bias_grad = lax.psum((gain_part, bias_part), ("ctx", "fsdp"))
    input_grad = grad_low.astype(jnp.float32) + input_part
    return (
        layer_output[None],
        input_grad[None],
        gain_grad,
        bias_grad,
        qkv_grad,
        up_grad,
        dense_grad,
        down_grad,
    )


def solution(mesh):
    return jax.shard_map(
        body,
        mesh=mesh,
        in_specs=(
            P("fsdp", "ctx", None),
            P("fsdp", "ctx", None),
            P(),
            P(),
            P("ctx", "fsdp"),
            P("ctx", "fsdp"),
            P("ctx", "fsdp"),
            P("ctx", "fsdp"),
        ),
        out_specs=(
            P("fsdp", "ctx", None),
            P("fsdp", "ctx", None),
            P(),
            P(),
            P("ctx", "fsdp"),
            P("ctx", "fsdp"),
            P("ctx", "fsdp"),
            P("ctx", "fsdp"),
        ),
        check_vma=False,
    )
```

profile of v0, /device:TPU:0, one launch (start us, length us, event | category | flops | bytes accessed | tf_op | source)
XLA Modules:
  0.0 8374.2 jit_solution(7402094966194372725)
XLA Ops:
  10.0 13.9 all-gather.25.cloned.1.call-done
  31.6 17.7 all-gather.17.cloned.1.call-done
  49.4 14.1 all-gather.29.cloned.1.call-done
  76.5 12.4 all-gather.19.cloned.1.call-done
  94.9 444.6 %all-gather.27.cloned.1.call-done = bf16[16,284,4672]{2,1,0:T(8,128)(2,1)} async-done(((bf16[1,284,4672]{2,1,0:T(8,128)(2,1)}), bf16[16,284,4672]{2,1,0:T(8,128)(2,1)}) %all-gather.27.cloned.1.call-update) | async-done | bytes 42459152 | tf_op jit(solution)/shard_map/all_gather | solution.py:62
  539.5 64.0 reshape.226
  603.5 26.1 fusion.70
  634.5 46.7 all_gather.43
  737.6 9.0 fusion.57
  746.6 72.6 while.146
  836.3 1326.4 %all-gather.33.cloned.1.call-done = bf16[16,284,18176]{2,1,0:T(8,128)(2,1)} async-done(((bf16[1,284,18176]{2,1,0:T(8,128)(2,1)}), bf16[16,284,18176]{2,1,0:T(8,128)(2,1)}) %all-gather.33.cloned.1.call-update) | async-done | bytes 165183504 | tf_op jit(solution)/shard_map/all_gather | solution.py:67
  2162.7 152.8 %reshape.232 = bf16[4544,18176]{1,0:T(8,128)(2,1)} reshape(bf16[16,284,18176]{2,1,0:T(8,128)(2,1)} %all-gather.33.cloned.1.call-done) | data formatting | bytes 330366976
  2315.5 66.3 multiply_convert_fusion
  2388.5 7.6 pad_maximum_fusion.1
  2396.2 203.2 %all-gather.31.cloned.1.call-done = bf16[16,284,4544]{2,1,0:T(8,128)(2,1)} async-done(((bf16[1,284,4544]{2,1,0:T(8,128)(2,1)}), bf16[16,284,4544]{2,1,0:T(8,128)(2,1)}) %all-gather.31.cloned.1.call-update) | async-done | bytes 41295888 | tf_op jit(solution)/shard_map/all_gather | solution.py:77
  2599.4 63.0 reshape.230
  2662.4 22.1 convolution_convert_fusion.2
  2699.1 97.4 %while.148 = (s32[]{:T(128)}, f32[2048,128]{0,1:T(8,128)S(1)}, f32[4,2272,64]{1,0,2:T(4,128)}, s32[4]{0:T(128)S(1)}, s32[]{:T(128)}, /*index=5*/bf16[4,2272,64]{...) while((s32[]{:T(128)}, f32[2048,128]{0,1:T(8,128)S(1)}, ...), condition=%wide.region_14.15_spmd, body=%wide.region_11.14_spmd.sunk | while | flops 1510556672 | bytes 51870676 | solution.py:238
  2704.1 8.3 while.151
  2713.0 10.5 dynamic_update_slice.56
  2728.4 8.3 while.151
  2737.3 10.6 dynamic_update_slice.56
  2752.8 8.3 while.151
  2761.7 10.6 dynamic_update_slice.56
  2777.1 8.3 while.151
  2786.0 10.5 dynamic_update_slice.56
  2797.8 36.2 all-to-all-start
  2834.0 9.4 reshape_reshape.10
  2859.8 1368.5 %all-gather.35.cloned.1.call-done = bf16[16,284,18176]{2,1,0:T(8,128)(2,1)} async-done(((bf16[1,284,18176]{2,1,0:T(8,128)(2,1)}), bf16[16,284,18176]{2,1,0:T(8,128)(2,1)}) %all-gather.35.cloned.1.call-update) | async-done | bytes 165183504 | tf_op jit(solution)/shard_map/all_gather | solution.py:83
  4228.3 150.5 %reshape.234 = bf16[4544,18176]{1,0:T(8,128)(2,1)} reshape(bf16[16,284,18176]{2,1,0:T(8,128)(2,1)} %all-gather.35.cloned.1.call-done) | data formatting | bytes 330366976
  4378.9 61.8 add_convert_fusion
  4454.8 61.6 all_to_all.40
  4517.5 1603.3 %all-gather.23.cloned.1.call-done = bf16[2048,22720]{0,1:T(8,128)(2,1)} async-done(((bf16[128,22720]{0,1:T(8,128)(2,1)}), bf16[2048,22720]{0,1:T(8,128)(2,1)}) %all-gather.23.cloned.1.call-update) | async-done | bytes 93061136 | tf_op jit(solution)/shard_map/all_gather | solution.py:94
  6120.8 42.7 fusion.46
  6163.4 19.0 copy.97
  6186.7 100.7 %all_to_all.41 = bf16[128,16,284]{0,2,1:T(8,128)(2,1)S(1)} all-to-all(bf16[128,16,284]{0,2,1:T(8,128)(2,1)S(1)} %add_convert_fusion.1), channel_id=1, replica_groups=mesh['ctx'=16,'fsdp'=2] {'ctx'}, dimensions={1} | all-to-all | bytes 2326528 | tf_op jit(solution)/shard_map/all_to_all | solution.py:90
  6288.3 1739.4 %all-gather.21.cloned.1.call-done = bf16[2048,22848]{0,1:T(8,128)(2,1)} async-done(((bf16[128,22848]{0,1:T(8,128)(2,1)}), bf16[2048,22848]{0,1:T(8,128)(2,1)}) %all-gather.21.cloned.1.call-update) | async-done | bytes 93585424 | tf_op jit(solution)/shard_map/all_gather | solution.py:94
  8027.7 48.0 convolution_convert_fusion.1
  8075.7 19.0 copy.95
  8097.6 23.6 fusion.75
  8121.3 60.0 fusion.76
  8181.3 22.7 fusion.71
  8208.7 41.7 all-reduce.4
  8254.6 59.2 fusion.55
  8315.5 8.0 slice.88
  8325.9 12.4 copy.124
  8341.8 8.0 slice.86
  8354.5 12.4 copy.122
  (334 shorter events, 353.6 us)
Async XLA Ops:
  7.2 16.7 all-gather.25.cloned.1.call-start
  7.9 41.5 all-gather.17.cloned.1.call-start
  8.6 54.9 all-gather.29.cloned.1.call-start
  9.4 79.4 all-gather.19.cloned.1.call-start
  10.0 529.5 %all-gather.27.cloned.1.call-start = ((), (), s32[]{:S(2)}) async-start(), calls=%async_computation.10 | async-start | bytes 46374912 | tf_op jit(solution)/shard_map/all_gather | solution.py:62
  31.6 2131.1 %all-gather.33.cloned.1.call-start = ((), (), s32[]{:S(2)}) async-start(), calls=%async_computation.13 | async-start | bytes 177979392 | tf_op jit(solution)/shard_map/all_gather | solution.py:67
  49.4 2550.0 %all-gather.31.cloned.1.call-start = ((), (), s32[]{:S(2)}) async-start(), calls=%async_computation.12 | async-start | bytes 45121536 | tf_op jit(solution)/shard_map/all_gather | solution.py:77
  69.4 19.7 copy-start.2
  76.4 15.2 copy-start.18
  76.4 15.2 copy-start.25
  76.4 4151.9 %all-gather.35.cloned.1.call-start = ((), (), s32[]{:S(2)}) async-start(), calls=%async_computation.14 | async-start | bytes 177979392 | tf_op jit(solution)/shard_map/all_gather | solution.py:83
  88.9 6031.9 %all-gather.23.cloned.1.call-start = ((), (), s32[]{:S(2)}) async-start(), calls=%async_computation.8 | async-start | bytes 98877440 | tf_op jit(solution)/shard_map/all_gather | solution.py:94
  89.8 1.8 copy-start.32
  629.6 1.4 copy-start.12
  634.5 79.6 copy-start.23
  634.5 91.2 %copy-start.21 = (f32[128,64]{0,1:T(8,128)}, f32[128,64]{0,1:T(8,128)S(1)}, u32[]{:S(2)}) copy-start(f32[128,64]{0,1:T(8,128)S(1)} %get-tuple-element.858) | copy-start | bytes 98308
  685.4 17.1 copy-start.13
  819.2 1496.3 %copy-start = (bf16[2048,128]{1,0:T(8,128)(2,1)}, bf16[2048,128]{1,0:T(8,128)(2,1)S(1)}, u32[]{:S(2)}) copy-start(bf16[2048,128]{1,0:T(8,128)(2,1)S(1)} %get-tuple-element.1500) | copy-start | bytes 1572868
  819.2 1496.3 %copy-start.6 = (bf16[4,2272,64]{2,1,0:T(8,128)(2,1)}, bf16[4,2272,64]{2,1,0:T(8,128)(2,1)S(1)}, u32[]{:S(2)}) copy-start(bf16[4,2272,64]{2,1,0:T(8,128)(2,1)S(1)} %get-tuple-element.1535) | copy-start | bytes 3489796
  2381.8 6.7 copy-start.17
  2396.2 266.2 %copy-start.9 = (bf16[1,128,4544]{1,2,0:T(8,128)(2,1)S(1)}, bf16[1,128,4544]{1,2,0:T(8,128)(2,1)}, u32[]{:S(2)}) copy-start(bf16[1,128,4544]{1,2,0:T(8,128)(2,1)} %param.19) | copy-start | bytes 3489796
  2686.4 12.7 copy-start.1
  2689.7 9.3 copy-start.7
  2796.5 46.9 copy-start.24
  2797.8 59.0 all-to-all-start
  2834.0 5193.7 %all-gather.21.cloned.1.call-start = ((), (), s32[]{:S(2)}) async-start(), calls=%async_computation.7 | async-start | bytes 99434496 | tf_op jit(solution)/shard_map/all_gather | solution.py:94
  2843.5 4.5 copy-start.5
  2843.5 4.5 copy-start.22
  2848.0 10.0 copy-start.27
  2851.3 1527.6 %copy-start.15 = (bf16[128,71,64]{0,2,1:T(8,128)(2,1)}, bf16[128,71,64]{0,2,1:T(8,128)(2,1)S(1)}, u32[]{:S(2)}) copy-start(bf16[128,71,64]{0,2,1:T(8,128)(2,1)S(1)} %copy.84) | copy-start | bytes 3489796
  2859.8 1519.0 %copy-start.10 = (bf16[1,128,4544]{1,2,0:T(8,128)(2,1)S(1)}, bf16[1,128,4544]{1,2,0:T(8,128)(2,1)}, u32[]{:S(2)}) copy-start(bf16[1,128,4544]{1,2,0:T(8,128)(2,1)} %param.19) | copy-start | bytes 3489796
  4440.6 6.7 copy-start.14
  4454.5 3859.3 %reduce-scatter.9.cloned.1.call-start = ((), (), s32[]{:S(2)}) async-start(), calls=%async_computation.16 | async-start | bytes 26173440
  6182.4 0.8 copy-start.19
  6182.4 1.5 copy-start.3
  6182.4 1.8 copy-start.33
  6182.4 1.8 copy-start.36
  6182.5 2155.8 %reduce-scatter.7.cloned.1.call-start = ((), (), s32[]{:S(2)}) async-start(), calls=%async_computation.15 | async-start | bytes 26320896
  8094.7 1.7 copy-start.8
  8121.2 60.0 copy-start.4
  8121.2 60.0 copy-start.16
  8121.3 60.0 copy-start.20
  8121.3 60.0 copy-start.29
  8121.3 60.0 copy-start.31
  8121.3 60.0 copy-start.34
  8181.3 22.8 copy-start.39
  8181.3 23.4 copy-start.37
  8181.3 69.1 copy-start.11
  (5 other events, 3.1 us)
Sparse Core Ops, SparseCore 0:
  9.5 14.3 all-gather.24
  25.4 23.8 all-gather.16
  50.9 12.5 all-gather.28
  64.9 23.8 all-gather.18
  92.0 447.3 all-gather.26
  542.2 1620.4 all-gather.32
  2166.1 433.2 all-gather.30
  2602.3 1626.0 all-gather.34
  4230.4 1890.3 all-gather.22
  6122.6 1904.9 all-gather.20
  8030.0 30.2 reduce-scatter.8
  8094.8 30.2 reduce-scatter.6
where the time goes:
time: 8390 us; the launch traced here: 8370 us
  waiting for transfers between devices  6750 us (80%)
  local copies, waits for them, and re-layouts  737 us (9%)
  matrix products  498 us (6%)
  blocking collectives  251 us (3%)
    all_gather x2, waiting for transfers between devices, grad_blocks(): lax.all_gather(right, 'ctx', axis=0, tiled=True)  3340 us
    all_gather x1, waiting for transfers between devices, fold_outputs(): lax.all_gather(second, 'ctx', axis=0, tiled=True)  1370 us
    all_gather x1, waiting for transfers between devices, fold_inputs(): lax.all_gather(second, 'ctx', axis=0, tiled=True)  1330 us
    unnamed x98, local copies, waits for them, and re-layouts  523 us
    all_gather x1, waiting for transfers between devices, fold_inputs(): lax.all_gather(first, 'ctx', axis=0, tiled=True)  445 us
    all_gather x1, waiting for transfers between devices, fold_outputs(): lax.all_gather(first, 'ctx', axis=0, tiled=True)  203 us
  transfers between devices with their start and end apart: 13, of which 11 were waited for; matrix products, arithmetic and copies ran while one was open for 15% of the time, Pallas kernels for 0%

commit v1 on v0

--- a/solution.py
+++ b/solution.py
@@ -9,6 +9,22 @@
 epsilon = 1e-05
 rope_base = 10000.0
 masked_score = -1e30
+
+
+def ring_gather(x, axis, dim):
+    ways, here, turn = (lax.axis_size(axis), lax.axis_index(axis), x.shape[dim])
+    dims = [n * ways if d == dim else n for d, n in enumerate(x.shape)]
+    full = lax.dynamic_update_slice_in_dim(jnp.zeros(dims, x.dtype), x, here * turn, axis=dim)
+    going_up = going_down = x
+    for far in range(1, ways // 2 + 1):
+        going_up = lax.ppermute(going_up, axis, [(d, (d + 1) % ways) for d in range(ways)])
+        full = lax.dynamic_update_slice_in_dim(full, going_up, (here - far) % ways * turn, axis=dim)
+        if 2 * far < ways:
+            going_down = lax.ppermute(going_down, axis, [(d, (d - 1) % ways) for d in range(ways)])
+            full = lax.dynamic_update_slice_in_dim(
+                full, going_down, (here + far) % ways * turn, axis=dim
+            )
+    return full
 
 
 def in_blocks(shard, dim, size):
@@ -90,10 +106,7 @@
     left_columns = lax.all_to_all(left, "ctx", split_axis=1, concat_axis=0, tiled=True)
     across = (((0,), (0,)), ((), ()))
     return lax.dot_general(
-        left_columns,
-        lax.all_gather(right, "ctx", axis=0, tiled=True),
-        across,
-        preferred_element_type=jnp.float32,
+        left_columns, ring_gather(right, "ctx", 0), across, preferred_element_type=jnp.float32
     )
 
 

time: 8390 us -> 8670 us (1.033)
  starting transfers between devices: 36.8 us -> 1500 us
  waiting for transfers between devices: 6750 us -> 5550 us
  local copies, waits for them, and re-layouts: 737 us -> 915 us
  blocking collectives: 251 us -> 90.1 us
    all_gather x2 -> x0, waiting for transfers between devices: 3340 us -> none  [grad_blocks(): lax.all_gather(right, 'ctx', axis=0, tiled=True)]
    ppermute x0 -> x30, waiting for transfers between devices: none -> 1960 us  [the longest x16 1810 us: ring_gather(): lax.ppermute(going_up, axis, [(d, (d + 1) % ways) for d in range(ways)])]
    ppermute x0 -> x30, starting transfers between devices: none -> 1380 us  [the longest x14 1370 us: ring_gather(): lax.ppermute(going_down, axis, [(d, (d - 1) % ways) for d in range(ways)])]
    all_gather x1, waiting for transfers between devices: 1370 us -> 1610 us  [fold_outputs(): lax.all_gather(second, 'ctx', axis=0, tiled=True)]
    all_gather x1, waiting for transfers between devices: 1330 us -> 1120 us  [fold_inputs(): lax.all_gather(second, 'ctx', axis=0, tiled=True)]
    all_gather x1, waiting for transfers between devices: 203 us -> 367 us  [fold_outputs(): lax.all_gather(first, 'ctx', axis=0, tiled=True)]
    all_to_all x2 -> x0, blocking collectives: 162 us -> none  [grad_blocks(): lax.all_to_all(left, 'ctx', split_axis=1, concat_axis=0, tiled=True)]
    dynamic_update_slice x0 -> x32, local copies, waits for them, and re-layouts: none -> 136 us  [the longest x16 71.4 us: ring_gather(): lax.dynamic_update_slice_in_dim(full, going_up, (here - far) % ways * tur...]
  transfers between devices with their start and end apart: 13 -> 43, of which waited for: 11 -> 20; matrix products, arithmetic and copies ran while one was open for 15% -> 17% of each run, Pallas kernels for 0% -> 0%
where the time goes in v1:
time: 8670 us; the launch traced here: 8650 us
  waiting for transfers between devices  5550 us (64%)
  starting transfers between devices  1500 us (17%)
  local copies, waits for them, and re-layouts  915 us (11%)
  matrix products  486 us (6%)
  blocking collectives  90.1 us (1%)
    ppermute x16, waiting for transfers between devices, ring_gather(): lax.ppermute(going_up, axis, [(d, (d + 1) % ways) for d in range(ways)])  1810 us
    all_gather x1, waiting for transfers between devices, fold_outputs(): lax.all_gather(second, 'ctx', axis=0, tiled=True)  1610 us
    ppermute x14, starting transfers between devices, ring_gather(): lax.ppermute(going_down, axis, [(d, (d - 1) % ways) for d in range(ways)])  1370 us
    all_gather x1, waiting for transfers between devices, fold_inputs(): lax.all_gather(second, 'ctx', axis=0, tiled=True)  1120 us
    unnamed x96, local copies, waits for them, and re-layouts  520 us
    all_gather x1, waiting for transfers between devices, fold_outputs(): lax.all_gather(first, 'ctx', axis=0, tiled=True)  367 us
    all_gather x1, waiting for transfers between devices, fold_inputs(): lax.all_gather(first, 'ctx', axis=0, tiled=True)  364 us
  transfers between devices with their start and end apart: 43, of which 20 were waited for; matrix products, arithmetic and copies ran while one was open for 17% of the time, Pallas kernels for 0%

profile of v1, /device:TPU:0, one launch (start us, length us, event | category | flops | bytes accessed | tf_op | source)
XLA Modules:
  0.0 8654.1 jit_solution(10347442615897035439)
XLA Ops:
  45.8 17.8 all-gather.15.cloned.1.call-done
  63.6 25.2 all-gather.17.cloned.1.call-done
  106.0 33.0 all-to-all-done.2
  139.0 21.0 all-to-all-start.1
  166.4 33.7 all-to-all-done.1
  203.4 367.1 %all-gather.25.cloned.1.call-done = bf16[16,284,4544]{2,1,0:T(8,128)(2,1)} async-done(((bf16[1,284,4544]{2,1,0:T(8,128)(2,1)}), bf16[16,284,4544]{2,1,0:T(8,128)(2,1)}) %all-gather.25.cloned.1.call-update) | async-done | bytes 41295888 | tf_op jit(solution)/shard_map/all_gather | solution.py:93
  570.5 57.9 reshape.230
  628.4 21.9 convolution_convert_fusion.2
  654.3 363.9 %all-gather.21.cloned.1.call-done = bf16[16,284,4672]{2,1,0:T(8,128)(2,1)} async-done(((bf16[1,284,4672]{2,1,0:T(8,128)(2,1)}), bf16[16,284,4672]{2,1,0:T(8,128)(2,1)}) %all-gather.21.cloned.1.call-update) | async-done | bytes 42459152 | tf_op jit(solution)/shard_map/all_gather | solution.py:78
  1018.2 64.0 reshape.226
  1082.2 26.1 fusion.70
  1113.2 46.2 all_gather.37
  1225.0 67.3 while.146
  1302.4 94.6 %while.148 = (s32[]{:T(128)}, f32[2048,128]{0,1:T(8,128)S(1)}, f32[4,2272,64]{1,0,2:T(4,128)}, s32[4]{0:T(128)S(1)}, s32[]{:T(128)}, /*index=5*/bf16[4,2272,64]{...) while((s32[]{:T(128)}, f32[2048,128]{0,1:T(8,128)S(1)}, ...), condition=%wide.region_14.15_spmd, body=%wide.region_11.14_spmd.sunk | while | flops 1510556672 | bytes 51870668 | solution.py:251
  1398.3 94.6 %all-to-all-start = ((bf16[16,128,128]{1,2,0:T(8,128)(2,1)}), bf16[16,128,128]{1,2,0:T(8,128)(2,1)}, u32[]{:S(2)}, u32[]{:S(2)}) async-start(bf16[16,128,128]{1,2,0:T(8,128)(2,1)} %copy.86), calls=%async_computation | async-start | bytes 1048576 | tf_op jit(solution)/shard_map/all_to_all | solution.py:38
  1526.5 1124.7 %all-gather.27.cloned.1.call-done = bf16[16,284,18176]{2,1,0:T(8,128)(2,1)} async-done(((bf16[1,284,18176]{2,1,0:T(8,128)(2,1)}), bf16[16,284,18176]{2,1,0:T(8,128)(2,1)}) %all-gather.27.cloned.1.call-update) | async-done | bytes 165183504 | tf_op jit(solution)/shard_map/all_gather | solution.py:83
  2651.2 158.0 %reshape.232 = bf16[4544,18176]{1,0:T(8,128)(2,1)} reshape(bf16[16,284,18176]{2,1,0:T(8,128)(2,1)} %all-gather.27.cloned.1.call-done) | data formatting | bytes 330366976
  2809.2 61.6 multiply_convert_fusion
  2888.7 1609.3 %all-gather.29.cloned.1.call-done = bf16[16,284,18176]{2,1,0:T(8,128)(2,1)} async-done(((bf16[1,284,18176]{2,1,0:T(8,128)(2,1)}), bf16[16,284,18176]{2,1,0:T(8,128)(2,1)}) %all-gather.29.cloned.1.call-update) | async-done | bytes 165183504 | tf_op jit(solution)/shard_map/all_gather | solution.py:99
  4498.0 148.5 %reshape.234 = bf16[4544,18176]{1,0:T(8,128)(2,1)} reshape(bf16[16,284,18176]{2,1,0:T(8,128)(2,1)} %all-gather.29.cloned.1.call-done) | data formatting | bytes 330366976
  4646.5 60.9 add_convert_fusion
  4721.8 28.7 broadcast_in_dim.104
  4756.8 29.0 broadcast_in_dim.103
  4806.8 41.7 collective-permute-done.1
  4848.5 251.2 %collective-permute-start.3 = (bf16[128,22848]{0,1:T(8,128)(2,1)S(1)}, bf16[128,22848]{0,1:T(8,128)(2,1)S(1)}, u32[]{:S(2)}, u32[]{:S(2)}) collective-permute-start(bf16[128,22848]{0,1:T(8,128)(2,1)S(1)} %collective-permute-done.1), channel_id=1, source_target_pairs={{0,30},{2,0},{4,2},{6,4},{8,6},{10,8},{12,10},{14,12},{16,14},{18,... | collective-permute-start | bytes 17547272 | tf_op jit(solution)/shard_map/ppermute | solution.py:23
  5105.6 244.2 %collective-permute-start.20 = (bf16[128,22720]{0,1:T(8,128)(2,1)}, bf16[128,22720]{0,1:T(8,128)(2,1)S(1)}, u32[]{:S(2)}, u32[]{:S(2)}) collective-permute-start(bf16[128,22720]{0,1:T(8,128)(2,1)} %collective-permute-done.18), channel_id=1, source_target_pairs={{0,30},{2,0},{4,2},{6,4},{8,6},{10,8},{12,10},{14,12},{16,14},{18,... | collective-permute-start | bytes 17448968 | tf_op jit(solution)/shard_map/ppermute | solution.py:23
  5362.3 237.3 %collective-permute-start.5 = (bf16[128,22848]{0,1:T(8,128)(2,1)S(1)}, bf16[128,22848]{0,1:T(8,128)(2,1)S(1)}, u32[]{:S(2)}, u32[]{:S(2)}) collective-permute-start(bf16[128,22848]{0,1:T(8,128)(2,1)S(1)} %collective-permute-done.3), channel_id=1, source_target_pairs={{0,30},{2,0},{4,2},{6,4},{8,6},{10,8},{12,10},{14,12},{16,14},{18,... | collective-permute-start | bytes 17547272 | tf_op jit(solution)/shard_map/ppermute | solution.py:23
  5602.6 244.3 %collective-permute-done.19 = bf16[128,22720]{0,1:T(8,128)(2,1)} collective-permute-done((bf16[128,22720]{0,1:T(8,128)(2,1)}, bf16[128,22720]{0,1:T(8,128)(2,1)}, u32[]{:S(2)}, u32[]{:S(2)}) %collective-permute-start.19) | collective-permute-done | bytes 5816352 | tf_op jit(solution)/shard_map/ppermute | solution.py:20
  5864.8 234.9 %collective-permute-start.7 = (bf16[128,22848]{0,1:T(8,128)(2,1)S(1)}, bf16[128,22848]{0,1:T(8,128)(2,1)S(1)}, u32[]{:S(2)}, u32[]{:S(2)}) collective-permute-start(bf16[128,22848]{0,1:T(8,128)(2,1)S(1)} %collective-permute-done.5), channel_id=1, source_target_pairs={{0,30},{2,0},{4,2},{6,4},{8,6},{10,8},{12,10},{14,12},{16,14},{18,... | collective-permute-start | bytes 17547272 | tf_op jit(solution)/shard_map/ppermute | solution.py:23
  6099.7 247.2 %collective-permute-done.21 = bf16[128,22720]{0,1:T(8,128)(2,1)S(1)} collective-permute-done((bf16[128,22720]{0,1:T(8,128)(2,1)}, bf16[128,22720]{0,1:T(8,128)(2,1)S(1)}, u32[]{:S(2)}, u32[]{:S(2)}) %collective-permute-start.21) | collective-permute-done | bytes 5816352 | tf_op jit(solution)/shard_map/ppermute | solution.py:20
  6361.5 359.8 %collective-permute-done.23 = bf16[128,22720]{0,1:T(8,128)(2,1)} collective-permute-done((bf16[128,22720]{0,1:T(8,128)(2,1)S(1)}, bf16[128,22720]{0,1:T(8,128)(2,1)}, u32[]{:S(2)}, u32[]{:S(2)}) %collective-permute-start.23) | collective-permute-done | bytes 5816352 | tf_op jit(solution)/shard_map/ppermute | solution.py:20
  6741.6 358.4 %collective-permute-done.25 = bf16[128,22720]{0,1:T(8,128)(2,1)S(1)} collective-permute-done((bf16[128,22720]{0,1:T(8,128)(2,1)}, bf16[128,22720]{0,1:T(8,128)(2,1)S(1)}, u32[]{:S(2)}, u32[]{:S(2)}) %collective-permute-start.25) | collective-permute-done | bytes 5816352 | tf_op jit(solution)/shard_map/ppermute | solution.py:20
  7108.6 116.6 %collective-permute-done.8 = bf16[128,22848]{0,1:T(8,128)(2,1)S(1)} collective-permute-done((bf16[128,22848]{0,1:T(8,128)(2,1)S(1)}, bf16[128,22848]{0,1:T(8,128)(2,1)S(1)}, u32[]{:S(2)}, u32[]{:S(2)}) %collective-permute-start.8) | collective-permute-done | bytes 5849120 | tf_op jit(solution)/shard_map/ppermute | solution.py:20
  7233.8 241.2 %collective-permute-start.28 = (bf16[128,22720]{0,1:T(8,128)(2,1)S(1)}, bf16[128,22720]{0,1:T(8,128)(2,1)S(1)}, u32[]{:S(2)}, u32[]{:S(2)}) collective-permute-start(bf16[128,22720]{0,1:T(8,128)(2,1)S(1)} %collective-permute-done.26), channel_id=1, source_target_pairs={{0,30},{2,0},{4,2},{6,4},{8,6},{10,8},{12,10},{14,12},{16,14},{18,... | collective-permute-start | bytes 17448968 | tf_op jit(solution)/shard_map/ppermute | solution.py:23
  7481.1 244.1 %collective-permute-done.10 = bf16[128,22848]{0,1:T(8,128)(2,1)} collective-permute-done((bf16[128,22848]{0,1:T(8,128)(2,1)S(1)}, bf16[128,22848]{0,1:T(8,128)(2,1)}, u32[]{:S(2)}, u32[]{:S(2)}) %collective-permute-start.10) | collective-permute-done | bytes 5849120 | tf_op jit(solution)/shard_map/ppermute | solution.py:20
  7733.7 116.1 %collective-permute-done.29 = bf16[128,22720]{0,1:T(8,128)(2,1)S(1)} collective-permute-done((bf16[128,22720]{0,1:T(8,128)(2,1)S(1)}, bf16[128,22720]{0,1:T(8,128)(2,1)S(1)}, u32[]{:S(2)}, u32[]{:S(2)}) %collective-permute-start.29) | collective-permute-done | bytes 5816352 | tf_op jit(solution)/shard_map/ppermute | solution.py:20
  7852.7 42.0 fusion.46
  7894.7 19.0 copy.97
  7926.3 128.3 %collective-permute-start.13 = (bf16[128,22848]{0,1:T(8,128)(2,1)}, bf16[128,22848]{0,1:T(8,128)(2,1)S(1)}, u32[]{:S(2)}, u32[]{:S(2)}) collective-permute-start(bf16[128,22848]{0,1:T(8,128)(2,1)} %collective-permute-done.11), channel_id=1, source_target_pairs={{0,30},{2,0},{4,2},{6,4},{8,6},{10,8},{12,10},{14,12},{16,14},{18,... | collective-permute-start | bytes 17547272 | tf_op jit(solution)/shard_map/ppermute | solution.py:23
  8075.1 105.3 %collective-permute-done.13 = bf16[128,22848]{0,1:T(8,128)(2,1)S(1)} collective-permute-done((bf16[128,22848]{0,1:T(8,128)(2,1)}, bf16[128,22848]{0,1:T(8,128)(2,1)S(1)}, u32[]{:S(2)}, u32[]{:S(2)}) %collective-permute-start.13) | collective-permute-done | bytes 5849120 | tf_op jit(solution)/shard_map/ppermute | solution.py:23
  8183.4 124.3 %collective-permute-done.14 = bf16[128,22848]{0,1:T(8,128)(2,1)S(1)} collective-permute-done((bf16[128,22848]{0,1:T(8,128)(2,1)}, bf16[128,22848]{0,1:T(8,128)(2,1)S(1)}, u32[]{:S(2)}, u32[]{:S(2)}) %collective-permute-start.14) | collective-permute-done | bytes 5849120 | tf_op jit(solution)/shard_map/ppermute | solution.py:20
  8310.6 42.7 convolution_convert_fusion.1
  8353.3 19.1 copy.95
  8375.3 23.4 fusion.75
  8398.8 60.3 fusion.76
  8459.2 22.7 fusion.71
  8486.5 43.8 all-reduce.4
  8534.6 59.1 fusion.55
  (422 shorter events, 685.7 us)
Async XLA Ops:
  7.2 16.5 all-gather.23.cloned.1.call-start
  7.9 30.1 all-gather.19.cloned.1.call-start
  8.6 54.9 all-gather.15.cloned.1.call-start
  9.4 79.4 all-gather.17.cloned.1.call-start
  10.0 560.6 %all-gather.25.cloned.1.call-start = ((), (), s32[]{:S(2)}) async-start(), calls=%async_computation.10 | async-start | bytes 45121536 | tf_op jit(solution)/shard_map/all_gather | solution.py:93
  31.8 986.4 %all-gather.21.cloned.1.call-start = ((), (), s32[]{:S(2)}) async-start(), calls=%async_computation.8 | async-start | bytes 46374912 | tf_op jit(solution)/shard_map/all_gather | solution.py:78
  45.7 2605.5 %all-gather.27.cloned.1.call-start = ((), (), s32[]{:S(2)}) async-start(), calls=%async_computation.11 | async-start | bytes 177979392 | tf_op jit(solution)/shard_map/all_gather | solution.py:83
  63.6 4434.4 %all-gather.29.cloned.1.call-start = ((), (), s32[]{:S(2)}) async-start(), calls=%async_computation.12 | async-start | bytes 177979392 | tf_op jit(solution)/shard_map/all_gather | solution.py:99
  90.0 49.0 all-to-all-start.2
  139.0 61.0 all-to-all-start.1
  1398.3 124.7 %all-to-all-start = ((bf16[16,128,128]{1,2,0:T(8,128)(2,1)}), bf16[16,128,128]{1,2,0:T(8,128)(2,1)}, u32[]{:S(2)}, u32[]{:S(2)}) async-start(bf16[16,128,128]{1,2,0:T(8,128)(2,1)} %copy.86), calls=%async_computation | async-start | bytes 1048576 | tf_op jit(solution)/shard_map/all_to_all | solution.py:38
  1492.9 7100.9 %reduce-scatter.9.cloned.1.call-start = ((), (), s32[]{:S(2)}) async-start(), calls=%async_computation.14 | async-start | bytes 26173440
  1523.0 1286.2 %copy-start.14 = (bf16[128,71,64]{0,2,1:T(8,128)(2,1)}, bf16[128,71,64]{0,2,1:T(8,128)(2,1)S(1)}, u32[]{:S(2)}) copy-start(bf16[128,71,64]{0,2,1:T(8,128)(2,1)S(1)} %copy.84) | copy-start | bytes 3489796
  1526.5 1282.7 %copy-start.19 = (bf16[128,4544]{0,1:T(8,128)(2,1)S(1)}, bf16[128,4544]{0,1:T(8,128)(2,1)}, u32[]{:S(2)}) copy-start(bf16[128,4544]{0,1:T(8,128)(2,1)} %add_convert_fusion.4.clone.4) | copy-start | bytes 3489796
  2884.7 1761.7 %copy-start.7 = (bf16[1,128,4544]{1,2,0:T(8,128)(2,1)S(1)}, bf16[1,128,4544]{1,2,0:T(8,128)(2,1)}, u32[]{:S(2)}) copy-start(bf16[1,128,4544]{1,2,0:T(8,128)(2,1)} %param.19) | copy-start | bytes 3489796
  2884.7 1904.1 %collective-permute-start.16 = (bf16[128,22720]{0,1:T(8,128)(2,1)}, bf16[128,22720]{0,1:T(8,128)(2,1)}, u32[]{:S(2)}, u32[]{:S(2)}) collective-permute-start(bf16[128,22720]{0,1:T(8,128)(2,1)} %bitcast.31), channel_id=1, source_target_pairs={{0,30},{2,0},{4,2},{6,4},{8,6},{10,8},{12,10},{14,12},{16,14},{18,... | collective-permute-start | bytes 17448968 | tf_op jit(solution)/shard_map/ppermute | solution.py:23
  2888.7 1905.6 %collective-permute-start.15 = (bf16[128,22720]{0,1:T(8,128)(2,1)}, bf16[128,22720]{0,1:T(8,128)(2,1)}, u32[]{:S(2)}, u32[]{:S(2)}) collective-permute-start(bf16[128,22720]{0,1:T(8,128)(2,1)} %bitcast.31), channel_id=1, source_target_pairs={{0,2},{2,4},{4,6},{6,8},{8,10},{10,12},{12,14},{14,16},{16,18},{18... | collective-permute-start | bytes 17448968 | tf_op jit(solution)/shard_map/ppermute | solution.py:20
  4719.5 129.0 %collective-permute-start.1 = (bf16[128,22848]{0,1:T(8,128)(2,1)S(1)}, bf16[128,22848]{0,1:T(8,128)(2,1)S(1)}, u32[]{:S(2)}, u32[]{:S(2)}) collective-permute-start(bf16[128,22848]{0,1:T(8,128)(2,1)S(1)} %bitcast.215), channel_id=1, source_target_pairs={{0,30},{2,0},{4,2},{6,4},{8,6},{10,8},{12,10},{14,12},{16,14},{18,... | collective-permute-start | bytes 17547272 | tf_op jit(solution)/shard_map/ppermute | solution.py:23
  4721.8 377.9 %collective-permute-start = (bf16[128,22848]{0,1:T(8,128)(2,1)S(1)}, bf16[128,22848]{0,1:T(8,128)(2,1)S(1)}, u32[]{:S(2)}, u32[]{:S(2)}) collective-permute-start(bf16[128,22848]{0,1:T(8,128)(2,1)S(1)} %bitcast.216), channel_id=1, source_target_pairs={{0,2},{2,4},{4,6},{6,8},{8,10},{10,12},{12,14},{14,16},{16,18},{18... | collective-permute-start | bytes 17547272 | tf_op jit(solution)/shard_map/ppermute | solution.py:20
  4788.8 316.8 %collective-permute-start.18 = (bf16[128,22720]{0,1:T(8,128)(2,1)}, bf16[128,22720]{0,1:T(8,128)(2,1)}, u32[]{:S(2)}, u32[]{:S(2)}) collective-permute-start(bf16[128,22720]{0,1:T(8,128)(2,1)} %collective-permute-done.16), channel_id=1, source_target_pairs={{0,30},{2,0},{4,2},{6,4},{8,6},{10,8},{12,10},{14,12},{16,14},{18,... | collective-permute-start | bytes 17448968 | tf_op jit(solution)/shard_map/ppermute | solution.py:23
  4794.3 555.5 %collective-permute-start.17 = (bf16[128,22720]{0,1:T(8,128)(2,1)}, bf16[128,22720]{0,1:T(8,128)(2,1)}, u32[]{:S(2)}, u32[]{:S(2)}) collective-permute-start(bf16[128,22720]{0,1:T(8,128)(2,1)} %collective-permute-done.15), channel_id=1, source_target_pairs={{0,2},{2,4},{4,6},{6,8},{8,10},{10,12},{12,14},{14,16},{16,18},{18... | collective-permute-start | bytes 17448968 | tf_op jit(solution)/shard_map/ppermute | solution.py:20
  4848.5 513.8 %collective-permute-start.3 = (bf16[128,22848]{0,1:T(8,128)(2,1)S(1)}, bf16[128,22848]{0,1:T(8,128)(2,1)S(1)}, u32[]{:S(2)}, u32[]{:S(2)}) collective-permute-start(bf16[128,22848]{0,1:T(8,128)(2,1)S(1)} %collective-permute-done.1), channel_id=1, source_target_pairs={{0,30},{2,0},{4,2},{6,4},{8,6},{10,8},{12,10},{14,12},{16,14},{18,... | collective-permute-start | bytes 17547272 | tf_op jit(solution)/shard_map/ppermute | solution.py:23
  5099.7 500.0 %collective-permute-start.2 = (bf16[128,22848]{0,1:T(8,128)(2,1)S(1)}, bf16[128,22848]{0,1:T(8,128)(2,1)S(1)}, u32[]{:S(2)}, u32[]{:S(2)}) collective-permute-start(bf16[128,22848]{0,1:T(8,128)(2,1)S(1)} %collective-permute-done), channel_id=1, source_target_pairs={{0,2},{2,4},{4,6},{6,8},{8,10},{10,12},{12,14},{14,16},{16,18},{18... | collective-permute-start | bytes 17547272 | tf_op jit(solution)/shard_map/ppermute | solution.py:20
  5105.6 746.8 %collective-permute-start.20 = (bf16[128,22720]{0,1:T(8,128)(2,1)}, bf16[128,22720]{0,1:T(8,128)(2,1)S(1)}, u32[]{:S(2)}, u32[]{:S(2)}) collective-permute-start(bf16[128,22720]{0,1:T(8,128)(2,1)} %collective-permute-done.18), channel_id=1, source_target_pairs={{0,30},{2,0},{4,2},{6,4},{8,6},{10,8},{12,10},{14,12},{16,14},{18,... | collective-permute-start | bytes 17448968 | tf_op jit(solution)/shard_map/ppermute | solution.py:23
  5349.8 497.1 %collective-permute-start.19 = (bf16[128,22720]{0,1:T(8,128)(2,1)}, bf16[128,22720]{0,1:T(8,128)(2,1)}, u32[]{:S(2)}, u32[]{:S(2)}) collective-permute-start(bf16[128,22720]{0,1:T(8,128)(2,1)} %collective-permute-done.17), channel_id=1, source_target_pairs={{0,2},{2,4},{4,6},{6,8},{8,10},{10,12},{12,14},{14,16},{16,18},{18... | collective-permute-start | bytes 17448968 | tf_op jit(solution)/shard_map/ppermute | solution.py:20
  5362.3 502.4 %collective-permute-start.5 = (bf16[128,22848]{0,1:T(8,128)(2,1)S(1)}, bf16[128,22848]{0,1:T(8,128)(2,1)S(1)}, u32[]{:S(2)}, u32[]{:S(2)}) collective-permute-start(bf16[128,22848]{0,1:T(8,128)(2,1)S(1)} %collective-permute-done.3), channel_id=1, source_target_pairs={{0,30},{2,0},{4,2},{6,4},{8,6},{10,8},{12,10},{14,12},{16,14},{18,... | collective-permute-start | bytes 17547272 | tf_op jit(solution)/shard_map/ppermute | solution.py:23
  5599.7 500.0 %collective-permute-start.4 = (bf16[128,22848]{0,1:T(8,128)(2,1)S(1)}, bf16[128,22848]{0,1:T(8,128)(2,1)S(1)}, u32[]{:S(2)}, u32[]{:S(2)}) collective-permute-start(bf16[128,22848]{0,1:T(8,128)(2,1)S(1)} %collective-permute-done.2), channel_id=1, source_target_pairs={{0,2},{2,4},{4,6},{6,8},{8,10},{10,12},{12,14},{14,16},{16,18},{18... | collective-permute-start | bytes 17547272 | tf_op jit(solution)/shard_map/ppermute | solution.py:20
  5846.9 500.0 %collective-permute-start.21 = (bf16[128,22720]{0,1:T(8,128)(2,1)}, bf16[128,22720]{0,1:T(8,128)(2,1)S(1)}, u32[]{:S(2)}, u32[]{:S(2)}) collective-permute-start(bf16[128,22720]{0,1:T(8,128)(2,1)} %collective-permute-done.19), channel_id=1, source_target_pairs={{0,2},{2,4},{4,6},{6,8},{8,10},{10,12},{12,14},{14,16},{16,18},{18... | collective-permute-start | bytes 17448968 | tf_op jit(solution)/shard_map/ppermute | solution.py:20
  5852.4 502.9 %collective-permute-start.22 = (bf16[128,22720]{0,1:T(8,128)(2,1)S(1)}, bf16[128,22720]{0,1:T(8,128)(2,1)S(1)}, u32[]{:S(2)}, u32[]{:S(2)}) collective-permute-start(bf16[128,22720]{0,1:T(8,128)(2,1)S(1)} %collective-permute-done.20), channel_id=1, source_target_pairs={{0,30},{2,0},{4,2},{6,4},{8,6},{10,8},{12,10},{14,12},{16,14},{18,... | collective-permute-start | bytes 17448968 | tf_op jit(solution)/shard_map/ppermute | solution.py:23
  5864.8 862.1 %collective-permute-start.7 = (bf16[128,22848]{0,1:T(8,128)(2,1)S(1)}, bf16[128,22848]{0,1:T(8,128)(2,1)S(1)}, u32[]{:S(2)}, u32[]{:S(2)}) collective-permute-start(bf16[128,22848]{0,1:T(8,128)(2,1)S(1)} %collective-permute-done.5), channel_id=1, source_target_pairs={{0,30},{2,0},{4,2},{6,4},{8,6},{10,8},{12,10},{14,12},{16,14},{18,... | collective-permute-start | bytes 17547272 | tf_op jit(solution)/shard_map/ppermute | solution.py:23
  6099.7 630.3 %collective-permute-start.6 = (bf16[128,22848]{0,1:T(8,128)(2,1)S(1)}, bf16[128,22848]{0,1:T(8,128)(2,1)S(1)}, u32[]{:S(2)}, u32[]{:S(2)}) collective-permute-start(bf16[128,22848]{0,1:T(8,128)(2,1)S(1)} %collective-permute-done.4), channel_id=1, source_target_pairs={{0,2},{2,4},{4,6},{6,8},{8,10},{10,12},{12,14},{14,16},{16,18},{18... | collective-permute-start | bytes 17547272 | tf_op jit(solution)/shard_map/ppermute | solution.py:20
  6346.9 374.4 %collective-permute-start.23 = (bf16[128,22720]{0,1:T(8,128)(2,1)S(1)}, bf16[128,22720]{0,1:T(8,128)(2,1)}, u32[]{:S(2)}, u32[]{:S(2)}) collective-permute-start(bf16[128,22720]{0,1:T(8,128)(2,1)S(1)} %collective-permute-done.21), channel_id=1, source_target_pairs={{0,2},{2,4},{4,6},{6,8},{8,10},{10,12},{12,14},{14,16},{16,18},{18... | collective-permute-start | bytes 17448968 | tf_op jit(solution)/shard_map/ppermute | solution.py:20
  6355.3 377.7 %collective-permute-start.24 = (bf16[128,22720]{0,1:T(8,128)(2,1)S(1)}, bf16[128,22720]{0,1:T(8,128)(2,1)S(1)}, u32[]{:S(2)}, u32[]{:S(2)}) collective-permute-start(bf16[128,22720]{0,1:T(8,128)(2,1)S(1)} %collective-permute-done.22), channel_id=1, source_target_pairs={{0,30},{2,0},{4,2},{6,4},{8,6},{10,8},{12,10},{14,12},{16,14},{18,... | collective-permute-start | bytes 17448968 | tf_op jit(solution)/shard_map/ppermute | solution.py:23
  6721.3 378.6 %collective-permute-start.25 = (bf16[128,22720]{0,1:T(8,128)(2,1)}, bf16[128,22720]{0,1:T(8,128)(2,1)S(1)}, u32[]{:S(2)}, u32[]{:S(2)}) collective-permute-start(bf16[128,22720]{0,1:T(8,128)(2,1)} %collective-permute-done.23), channel_id=1, source_target_pairs={{0,2},{2,4},{4,6},{6,8},{8,10},{10,12},{12,14},{14,16},{16,18},{18... | collective-permute-start | bytes 17448968 | tf_op jit(solution)/shard_map/ppermute | solution.py:20
  6726.9 503.7 %collective-permute-start.9 = (bf16[128,22848]{0,1:T(8,128)(2,1)S(1)}, bf16[128,22848]{0,1:T(8,128)(2,1)}, u32[]{:S(2)}, u32[]{:S(2)}) collective-permute-start(bf16[128,22848]{0,1:T(8,128)(2,1)S(1)} %collective-permute-done.7), channel_id=1, source_target_pairs={{0,30},{2,0},{4,2},{6,4},{8,6},{10,8},{12,10},{14,12},{16,14},{18,... | collective-permute-start | bytes 17547272 | tf_op jit(solution)/shard_map/ppermute | solution.py:23
  6730.0 495.2 %collective-permute-start.8 = (bf16[128,22848]{0,1:T(8,128)(2,1)S(1)}, bf16[128,22848]{0,1:T(8,128)(2,1)S(1)}, u32[]{:S(2)}, u32[]{:S(2)}) collective-permute-start(bf16[128,22848]{0,1:T(8,128)(2,1)S(1)} %collective-permute-done.6), channel_id=1, source_target_pairs={{0,2},{2,4},{4,6},{6,8},{8,10},{10,12},{12,14},{14,16},{16,18},{18... | collective-permute-start | bytes 17547272 | tf_op jit(solution)/shard_map/ppermute | solution.py:20
  6733.0 500.8 %collective-permute-start.26 = (bf16[128,22720]{0,1:T(8,128)(2,1)S(1)}, bf16[128,22720]{0,1:T(8,128)(2,1)S(1)}, u32[]{:S(2)}, u32[]{:S(2)}) collective-permute-start(bf16[128,22720]{0,1:T(8,128)(2,1)S(1)} %collective-permute-done.24), channel_id=1, source_target_pairs={{0,30},{2,0},{4,2},{6,4},{8,6},{10,8},{12,10},{14,12},{16,14},{18,... | collective-permute-start | bytes 17448968 | tf_op jit(solution)/shard_map/ppermute | solution.py:23
  7099.9 378.1 %collective-permute-start.27 = (bf16[128,22720]{0,1:T(8,128)(2,1)S(1)}, bf16[128,22720]{0,1:T(8,128)(2,1)S(1)}, u32[]{:S(2)}, u32[]{:S(2)}) collective-permute-start(bf16[128,22720]{0,1:T(8,128)(2,1)S(1)} %collective-permute-done.25), channel_id=1, source_target_pairs={{0,2},{2,4},{4,6},{6,8},{8,10},{10,12},{12,14},{14,16},{16,18},{18... | collective-permute-start | bytes 17448968 | tf_op jit(solution)/shard_map/ppermute | solution.py:20
  7225.2 252.8 %copy-start.12 = (bf16[128,22848]{0,1:T(8,128)(2,1)}, bf16[128,22848]{0,1:T(8,128)(2,1)S(1)}, u32[]{:S(2)}) copy-start(bf16[128,22848]{0,1:T(8,128)(2,1)S(1)} %collective-permute-done.8) | copy-start | bytes 17547268
  7225.2 500.0 %collective-permute-start.10 = (bf16[128,22848]{0,1:T(8,128)(2,1)S(1)}, bf16[128,22848]{0,1:T(8,128)(2,1)}, u32[]{:S(2)}, u32[]{:S(2)}) collective-permute-start(bf16[128,22848]{0,1:T(8,128)(2,1)S(1)} %collective-permute-done.8), channel_id=1, source_target_pairs={{0,2},{2,4},{4,6},{6,8},{8,10},{10,12},{12,14},{14,16},{16,18},{18... | collective-permute-start | bytes 17547272 | tf_op jit(solution)/shard_map/ppermute | solution.py:20
  7230.6 695.6 %collective-permute-start.11 = (bf16[128,22848]{0,1:T(8,128)(2,1)}, bf16[128,22848]{0,1:T(8,128)(2,1)}, u32[]{:S(2)}, u32[]{:S(2)}) collective-permute-start(bf16[128,22848]{0,1:T(8,128)(2,1)} %collective-permute-done.9), channel_id=1, source_target_pairs={{0,30},{2,0},{4,2},{6,4},{8,6},{10,8},{12,10},{14,12},{16,14},{18,... | collective-permute-start | bytes 17547272 | tf_op jit(solution)/shard_map/ppermute | solution.py:23
  7233.8 496.9 %collective-permute-start.28 = (bf16[128,22720]{0,1:T(8,128)(2,1)S(1)}, bf16[128,22720]{0,1:T(8,128)(2,1)S(1)}, u32[]{:S(2)}, u32[]{:S(2)}) collective-permute-start(bf16[128,22720]{0,1:T(8,128)(2,1)S(1)} %collective-permute-done.26), channel_id=1, source_target_pairs={{0,30},{2,0},{4,2},{6,4},{8,6},{10,8},{12,10},{14,12},{16,14},{18,... | collective-permute-start | bytes 17448968 | tf_op jit(solution)/shard_map/ppermute | solution.py:23
  7478.0 371.8 %collective-permute-start.29 = (bf16[128,22720]{0,1:T(8,128)(2,1)S(1)}, bf16[128,22720]{0,1:T(8,128)(2,1)S(1)}, u32[]{:S(2)}, u32[]{:S(2)}) collective-permute-start(bf16[128,22720]{0,1:T(8,128)(2,1)S(1)} %collective-permute-done.27), channel_id=1, source_target_pairs={{0,2},{2,4},{4,6},{6,8},{8,10},{10,12},{12,14},{14,16},{16,18},{18... | collective-permute-start | bytes 17448968 | tf_op jit(solution)/shard_map/ppermute | solution.py:20
  7725.2 336.5 %collective-permute-start.12 = (bf16[128,22848]{0,1:T(8,128)(2,1)}, bf16[128,22848]{0,1:T(8,128)(2,1)}, u32[]{:S(2)}, u32[]{:S(2)}) collective-permute-start(bf16[128,22848]{0,1:T(8,128)(2,1)} %collective-permute-done.10), channel_id=1, source_target_pairs={{0,2},{2,4},{4,6},{6,8},{8,10},{10,12},{12,14},{14,16},{16,18},{18... | collective-permute-start | bytes 17547272 | tf_op jit(solution)/shard_map/ppermute | solution.py:20
  7913.8 704.5 %reduce-scatter.7.cloned.1.call-start = ((), (), s32[]{:S(2)}) async-start(), calls=%async_computation.13 | async-start | bytes 26320896
  7926.3 254.1 %collective-permute-start.13 = (bf16[128,22848]{0,1:T(8,128)(2,1)}, bf16[128,22848]{0,1:T(8,128)(2,1)S(1)}, u32[]{:S(2)}, u32[]{:S(2)}) collective-permute-start(bf16[128,22848]{0,1:T(8,128)(2,1)} %collective-permute-done.11), channel_id=1, source_target_pairs={{0,30},{2,0},{4,2},{6,4},{8,6},{10,8},{12,10},{14,12},{16,14},{18,... | collective-permute-start | bytes 17547272 | tf_op jit(solution)/shard_map/ppermute | solution.py:23
  8061.7 246.0 %collective-permute-start.14 = (bf16[128,22848]{0,1:T(8,128)(2,1)}, bf16[128,22848]{0,1:T(8,128)(2,1)S(1)}, u32[]{:S(2)}, u32[]{:S(2)}) collective-permute-start(bf16[128,22848]{0,1:T(8,128)(2,1)} %collective-permute-done.12), channel_id=1, source_target_pairs={{0,2},{2,4},{4,6},{6,8},{8,10},{10,12},{12,14},{14,16},{16,18},{18... | collective-permute-start | bytes 17547272 | tf_op jit(solution)/shard_map/ppermute | solution.py:20
  8075.1 235.5 %copy-start.17 = (bf16[36,8,16,128]{3,1,2,0:T(8,128)(2,1)S(1)}, bf16[36,8,16,128]{3,1,2,0:T(8,128)(2,1)}, u32[]{:S(2)}) copy-start(bf16[36,8,16,128]{3,1,2,0:T(8,128)(2,1)} %copy.115) | copy-start | bytes 3538948
  (34 other events, 1404.0 us)
Sparse Core Ops, SparseCore 0:
  9.5 14.0 all-gather.22
  25.2 12.7 all-gather.18
  39.6 23.8 all-gather.14
  64.9 23.8 all-gather.16
  92.0 478.4 all-gather.24
  573.8 444.3 all-gather.20
  1021.1 1630.0 all-gather.26
  2654.1 1843.8 all-gather.28
  7913.9 155.5 reduce-scatter.8
  8372.5 30.8 reduce-scatter.6
